TPU v7x, 32 devices: a whole 2x2x4 slice. The times are simulated.
32 devices in a mesh: near: 2 (over x), row: 4 (over z), col: 4 (over y, core).
Axes of the slice: x: 2, y: 2, z: 4, core: 2. Of those that a mesh axis runs over, the one named last changes fastest.
Arguments:
- right_side: float32 [32, 512, 128], P(('near', 'row', 'col')), may hold values from -6 to 6
- start_guess: float32 [32, 512, 128], P(('near', 'row', 'col')), may hold values from -6 to 6
- near_tiles: bfloat16 [32, 7, 512, 512], P(('near', 'row', 'col')), may hold values from -0.09375 to 0.09375
- tile_scales: float32 [32, 7], P(('near', 'row', 'col')), may hold values from 0.3 to 3
- neighbours: int32 [32, 7], P(('near', 'row', 'col')), may hold values from 0 to 31, as said below
- source_cluster_basis: bfloat16 [32, 512, 64], P(('near', 'row', 'col')), may hold values from -0.25 to 0.25
- basis_out: bfloat16 [32, 512, 64], P(('near', 'row', 'col')), may hold values from -0.75 to 0.75
- couplings: bfloat16 [32, 32, 64, 64], P(('near', 'row'), 'col'), may hold values from -0.125 to 0.125
Outputs:
- solution_field: float32 [32, 512, 128], P(('near', 'row', 'col'))
- residual: float32 [32, 512, 128], P(('near', 'row', 'col'))
Inputs may be any that keep to these rules, and one draw needn't show every extreme that they name: `neighbours`: row t names 7 different clusters, each within 4 of t in the wrapped cluster order.
All inputs are finite; a program needn't handle non-finite values.
Results may differ from a plain program's by a relative error of at most 0.0051.
Values may be sent and summed in bfloat16 or wider, within the bound.
A program may use at most 64 MiB of HBM per device.

v0:
```python
import jax
import jax.numpy as jnp
from jax import lax
from jax.sharding import PartitionSpec as P

REACH = 4
ITERS = 2


damping = 0.5


def shifted(value, axis, steps):
    count = lax.axis_size(axis)
    pairs = [(source, (source + steps) % count) for source in range(count)]
    return lax.ppermute(value, axis, pairs)


def shards(
    right_side,
    start_guess,
    near_tiles,
    tile_scales,
    neighbours,
    source_cluster_basis,
    basis_out,
    couplings,
):
    local_count = right_side.shape[0]
    clusters = local_count * lax.axis_size(("near", "row", "col"))
    col_count = lax.axis_size("col")
    col_index = lax.axis_index("col")
    group_index = lax.axis_index(("near", "row"))
    device = lax.axis_index(("near", "row", "col"))
    shift_count = REACH // local_count
    anchor_cluster = device * local_count + jnp.arange(local_count, dtype=jnp.int32)
    offsets = jnp.mod(neighbours - anchor_cluster[:, None] + REACH, clusters) - REACH
    window_rows = (jnp.arange(local_count, dtype=jnp.int32)[:, None] + REACH + offsets).reshape(-1)
    block_targets = group_index * couplings.shape[0] + jnp.arange(
        couplings.shape[0], dtype=jnp.int32
    )
    block_slots = col_index * couplings.shape[1] + jnp.arange(couplings.shape[1], dtype=jnp.int32)
    per_col = clusters // col_count
    within = block_slots % per_col
    column = block_slots // per_col
    distance = jnp.mod(
        block_targets[:, None]
        - ((within // local_count * col_count + column) * local_count + within % local_count)[
            None, :
        ],
        clusters,
    )
    admitted = (jnp.minimum(distance, clusters - distance) > REACH).astype(jnp.bfloat16)
    masked_values = couplings * admitted[:, :, None, None]
    iterate = start_guess
    residual = right_side
    for sweep in range(ITERS):
        coarse_level = iterate.astype(jnp.bfloat16)
        pieces = [coarse_level]
        for operate_distance in range(1, shift_count + 1):
            lower_part = shifted(coarse_level, ("near", "row", "col"), operate_distance)
            upper_part = shifted(coarse_level, ("near", "row", "col"), -operate_distance)
            pieces = [lower_part] + pieces + [upper_part]
        extended = jnp.concatenate(pieces, axis=0)
        nearby = jnp.take(extended, window_rows, axis=0).reshape(
            (local_count, near_tiles.shape[1]) + coarse_level.shape[1:]
        )
        basis_products = jnp.einsum(
            "ijkl,ijlc->ijkc", near_tiles, nearby, preferred_element_type=jnp.float32
        )
        near_term = jnp.sum(basis_products * tile_scales[:, :, None, None], axis=1)
        expansion_coefficients = jnp.einsum(
            "ilr,ilc->irc", source_cluster_basis, coarse_level, preferred_element_type=jnp.float32
        ).astype(jnp.bfloat16)
        partial_coefs = jnp.einsum(
            "lqsx,qxp->lsp",
            masked_values,
            lax.all_gather(expansion_coefficients, ("near", "row"), axis=0, tiled=True),
            preferred_element_type=jnp.float32,
        )
        farfield_coefficients = lax.psum_scatter(
            partial_coefs, "col", scatter_dimension=0, tiled=True
        )
        far_term = jnp.einsum(
            "ila,iac->ilc",
            basis_out,
            farfield_coefficients.astype(jnp.bfloat16),
            preferred_element_type=jnp.float32,
        )
        residual = right_side - (iterate + near_term + far_term)
        iterate = iterate + damping * residual
    return (iterate, residual)


def solution(mesh):
    in_specs = (
        P(("near", "row", "col"), None, None),
        P(("near", "row", "col"), None, None),
        P(("near", "row", "col"), None, None, None),
        P(("near", "row", "col"), None),
        P(("near", "row", "col"), None),
        P(("near", "row", "col"), None, None),
        P(("near", "row", "col"), None, None),
        P(("near", "row"), "col", None, None),
    )
    out_specs = (P(("near", "row", "col"), None, None), P(("near", "row", "col"), None, None))
    return jax.shard_map(shards, mesh=mesh, in_specs=in_specs, out_specs=out_specs, check_vma=False)
```

profile of v0, /device:TPU:0, one launch (start us, length us, event | category | flops | bytes accessed | tf_op | source)
XLA Modules:
  0.0 137.9 jit_solution(12203947346635375188)
XLA Ops:
  7.2 0.0 copy-start
  7.2 0.0 copy-start.1
  7.2 0.0 copy-start.4
  7.2 0.0 reduce-scatter.3.cloned.1.call-start
  7.3 1.0 convert_element_type.34
  8.3 3.1 %collective-permute-start = (bf16[1,512,128]{2,1,0:T(8,128)(2,1)S(1)}, bf16[1,512,128]{2,1,0:T(8,128)(2,1)S(1)}, u32[]{:S(2)}, u32[]{:S(2)}) collective-permute-start(bf16[1,512,128]{2,1,0:T(8,128)(2,1)S(1)} %convert_element_type.34), channel_id=1, source_target_pairs={{0,4},{1,5},{2,6},{3,7},{4,8},{5,9},{6,10},{7,11},{8,12},{9,13},{1... | collective-permute-start | bytes 393224 | tf_op jit(solution)/shard_map/ppermute | solution.py:16
  11.4 0.7 collective-permute-start.1
  12.1 1.5 %collective-permute-start.2 = (bf16[1,512,128]{2,1,0:T(8,128)(2,1)S(1)}, bf16[1,512,128]{2,1,0:T(8,128)(2,1)S(1)}, u32[]{:S(2)}, u32[]{:S(2)}) collective-permute-start(bf16[1,512,128]{2,1,0:T(8,128)(2,1)S(1)} %convert_element_type.34), channel_id=1, source_target_pairs={{0,2},{1,3},{2,4},{3,5},{4,6},{5,7},{6,8},{7,9},{8,10},{9,11},{10,... | collective-permute-start | bytes 393224 | tf_op jit(solution)/shard_map/ppermute | solution.py:16
  13.6 0.7 collective-permute-start.3
  14.3 4.6 %collective-permute-start.4 = (bf16[1,512,128]{2,1,0:T(8,128)(2,1)S(1)}, bf16[1,512,128]{2,1,0:T(8,128)(2,1)S(1)}, u32[]{:S(2)}, u32[]{:S(2)}) collective-permute-start(bf16[1,512,128]{2,1,0:T(8,128)(2,1)S(1)} %convert_element_type.34), channel_id=1, source_target_pairs={{0,31},{1,0},{2,1},{3,2},{4,3},{5,4},{6,5},{7,6},{8,7},{9,8},{10,9... | collective-permute-start | bytes 393224 | tf_op jit(solution)/shard_map/ppermute | solution.py:16
  19.0 1.0 convolution_convert_fusion.1
  20.0 30.8 %all-gather = bf16[512,128]{1,0:T(8,128)(2,1)S(1)} all-gather(bf16[64,128]{1,0:T(8,128)(2,1)S(1)} %convolution_convert_fusion.1), channel_id=2, replica_groups=mesh['near'=2,'row'=4,'col'=4] {'near','row'}, dimensions={0}, use_global_device_ids=true | all-gather | bytes 147456 | tf_op jit(solution)/shard_map/all_gather | solution.py:78
  50.8 0.1 fusion.37
  50.8 2.1 %convolution_bitcast_fusion.3 = f32[4,64,128]{2,1,0:T(8,128)} fusion(bf16[8,64,128,1]{2,1,0,3:T(8,128)(2,1)S(1)} %bitcast.93, bf16[4,8,64,64]{3,2,1,0:T(8,128)(2,1)} %param.17, bf16[4,8]{1,0:T(4,128)(2,1)S(1)} %fusion.37), kind=kOutput, calls=%fused_computation.17 | convolution fusion | flops 33685504 | bytes 524352 | tf_op jit(solution)/shard_map/lqsx,qxp->lsp/dot_general | solution.py:75
  52.9 0.0 reduce-scatter.3.cloned.1.call-update
  52.9 0.0 reduce-scatter.5.cloned.1.call-start
  53.0 0.0 copy-done.4
  53.0 0.1 copy.13
  53.2 0.0 copy-done.2
  53.2 0.1 copy.12
  53.3 0.0 collective-permute-done
  53.3 0.7 collective-permute-start.5
  54.0 0.0 collective-permute-done.1
  54.0 0.1 collective-permute-start.6
  54.1 0.0 collective-permute-done.2
  54.1 0.6 collective-permute-start.7
  54.7 0.0 collective-permute-done.3
  54.8 0.0 collective-permute-done.4
  54.8 4.8 %collective-permute-done.5 = bf16[1,512,128]{2,1,0:T(8,128)(2,1)S(1)} collective-permute-done((bf16[1,512,128]{2,1,0:T(8,128)(2,1)S(1)}, bf16[1,512,128]{2,1,0:T(8,128)(2,1)S(1)}, u32[]{:S(2)}, u32[]{:S(2)}) %collective-permute-start.5) | collective-permute-done | bytes 131104 | tf_op jit(solution)/shard_map/ppermute | solution.py:16
  59.6 0.0 copy-start.6
  59.7 0.4 collective-permute-done.6
  60.0 2.6 %collective-permute-done.7 = bf16[1,512,128]{2,1,0:T(8,128)(2,1)S(1)} collective-permute-done((bf16[1,512,128]{2,1,0:T(8,128)(2,1)S(1)}, bf16[1,512,128]{2,1,0:T(8,128)(2,1)S(1)}, u32[]{:S(2)}, u32[]{:S(2)}) %collective-permute-start.7) | collective-permute-done | bytes 131104 | tf_op jit(solution)/shard_map/ppermute | solution.py:16
  62.6 0.7 gather_fusion
  63.4 3.5 %multiply_reduce_fusion.1 = f32[128,512]{1,0:T(8,128)S(1)} fusion(bf16[1,7,512,512]{3,2,1,0:T(8,128)(2,1)} %param.12, bf16[7,512,128]{2,1,0:T(8,128)(2,1)S(1)} %gather_fusion, f32[7]{0:T(128)S(1)} %bitcast.95, pred[7]{0:T(512)(128)(4,1)S(1)} %get-tuple-element.5), kind=kOutput, calls=%fused_computation.7 | convolution fusion | flops 471072768 | bytes 4849699 | tf_op jit(solution)/shard_map/ijkl,ijlc->ijkc/dot_general | solution.py:68
  66.8 0.0 copy-start.3
  66.8 0.0 copy-start.5
  66.9 3.1 %reduce-scatter.3.cloned.1.call-done = f32[1,64,128]{2,1,0:T(8,128)} async-done(((f32[4,64,128]{2,1,0:T(8,128)}), f32[1,64,128]{2,1,0:T(8,128)}) %reduce-scatter.3.cloned.1.call-update) | async-done | bytes 32784 | tf_op jit(solution)/shard_map/reduce_scatter | solution.py:81
  70.0 1.0 fusion.44
  71.0 1.5 %collective-permute-start.8 = (bf16[1,512,128]{1,2,0:T(8,128)(2,1)S(1)}, bf16[1,512,128]{1,2,0:T(8,128)(2,1)S(1)}, u32[]{:S(2)}, u32[]{:S(2)}) collective-permute-start(bf16[1,512,128]{1,2,0:T(8,128)(2,1)S(1)} %get-tuple-element.7), channel_id=1, source_target_pairs={{0,4},{1,5},{2,6},{3,7},{4,8},{5,9},{6,10},{7,11},{8,12},{9,13},{1... | collective-permute-start | bytes 393224 | tf_op jit(solution)/shard_map/ppermute | solution.py:16
  72.5 0.0 collective-permute-start.9
  72.5 1.6 %collective-permute-start.10 = (bf16[1,512,128]{1,2,0:T(8,128)(2,1)S(1)}, bf16[1,512,128]{1,2,0:T(8,128)(2,1)S(1)}, u32[]{:S(2)}, u32[]{:S(2)}) collective-permute-start(bf16[1,512,128]{1,2,0:T(8,128)(2,1)S(1)} %get-tuple-element.7), channel_id=1, source_target_pairs={{0,2},{1,3},{2,4},{3,5},{4,6},{5,7},{6,8},{7,9},{8,10},{9,11},{10,... | collective-permute-start | bytes 393224 | tf_op jit(solution)/shard_map/ppermute | solution.py:16
  74.1 0.3 collective-permute-start.11
  74.4 5.0 %collective-permute-start.12 = (bf16[1,512,128]{1,2,0:T(8,128)(2,1)S(1)}, bf16[1,512,128]{1,2,0:T(8,128)(2,1)S(1)}, u32[]{:S(2)}, u32[]{:S(2)}) collective-permute-start(bf16[1,512,128]{1,2,0:T(8,128)(2,1)S(1)} %get-tuple-element.7), channel_id=1, source_target_pairs={{0,31},{1,0},{2,1},{3,2},{4,3},{5,4},{6,5},{7,6},{8,7},{9,8},{10,9... | collective-permute-start | bytes 393224 | tf_op jit(solution)/shard_map/ppermute | solution.py:16
  79.4 0.2 fusion.14
  79.6 30.8 %all-gather.1 = bf16[512,128]{1,0:T(8,128)(2,1)S(1)} all-gather(bf16[64,128]{1,0:T(8,128)(2,1)S(1)} %fusion.14), channel_id=3, replica_groups=mesh['near'=2,'row'=4,'col'=4] {'near','row'}, dimensions={0}, use_global_device_ids=true | all-gather | bytes 147456 | tf_op jit(solution)/shard_map/all_gather | solution.py:78
  110.4 1.0 convolution_bitcast_fusion.2
  111.4 0.0 reduce-scatter.5.cloned.1.call-update
  111.4 0.0 collective-permute-done.8
  111.4 0.5 collective-permute-start.13
  112.0 0.0 collective-permute-done.9
  112.0 0.1 collective-permute-start.14
  112.1 0.0 collective-permute-done.10
  112.1 0.9 collective-permute-start.15
  113.0 0.0 collective-permute-done.11
  113.1 0.0 collective-permute-done.12
  113.1 4.8 %collective-permute-done.13 = bf16[1,512,128]{1,2,0:T(8,128)(2,1)S(1)} collective-permute-done((bf16[1,512,128]{1,2,0:T(8,128)(2,1)S(1)}, bf16[1,512,128]{1,2,0:T(8,128)(2,1)S(1)}, u32[]{:S(2)}, u32[]{:S(2)}) %collective-permute-start.13) | collective-permute-done | bytes 131104 | tf_op jit(solution)/shard_map/ppermute | solution.py:16
  117.9 0.0 collective-permute-done.14
  117.9 3.2 %collective-permute-done.15 = bf16[1,512,128]{1,2,0:T(8,128)(2,1)S(1)} collective-permute-done((bf16[1,512,128]{1,2,0:T(8,128)(2,1)S(1)}, bf16[1,512,128]{1,2,0:T(8,128)(2,1)S(1)}, u32[]{:S(2)}, u32[]{:S(2)}) %collective-permute-start.15) | collective-permute-done | bytes 131104 | tf_op jit(solution)/shard_map/ppermute | solution.py:16
  121.1 0.6 gather_fusion.1
  121.7 3.4 %multiply_reduce_fusion = f32[128,512]{1,0:T(8,128)S(1)} fusion(bf16[1,7,512,512]{3,2,1,0:T(8,128)(2,1)} %param.12, bf16[7,512,128]{1,2,0:T(8,128)(2,1)S(1)} %gather_fusion.1, f32[7]{0:T(128)S(1)} %bitcast.96, pred[7]{0:T(512)(128)(4,1)S(1)} %get-tuple-element.5), kind=kOutput, calls=%fused_computation.6 | convolution fusion | flops 471072768 | bytes 4849699 | tf_op jit(solution)/shard_map/ijkl,ijlc->ijkc/dot_general | solution.py:68
  125.2 3.3 %reduce-scatter.5.cloned.1.call-done = f32[1,64,128]{2,1,0:T(8,128)} async-done(((f32[4,64,128]{2,1,0:T(8,128)}), f32[1,64,128]{2,1,0:T(8,128)}) %reduce-scatter.5.cloned.1.call-update) | async-done | bytes 32784 | tf_op jit(solution)/shard_map/reduce_scatter | solution.py:81
  128.4 1.0 multiply_add_fusion
  129.4 0.8 copy.15
  130.2 0.8 copy.16
  (28 shorter events, 0.3 us)
Async XLA Ops:
  7.2 62.8 %copy-start = (bf16[1,512,64]{1,2,0:T(8,128)(2,1)S(1)}, bf16[1,512,64]{1,2,0:T(8,128)(2,1)}, u32[]{:S(2)}) copy-start(bf16[1,512,64]{1,2,0:T(8,128)(2,1)} %param.16) | copy-start | bytes 196612
  7.2 45.8 %copy-start.1 = (f32[1,512,128]{2,1,0:T(8,128)S(1)}, f32[1,512,128]{2,1,0:T(8,128)}, u32[]{:S(2)}) copy-start(f32[1,512,128]{2,1,0:T(8,128)} %param.11) | copy-start | bytes 786436
  7.2 45.8 %copy-start.4 = (s32[1,7]{1,0:T(1,128)S(1)}, s32[1,7]{1,0:T(1,128)}, u32[]{:S(2)}) copy-start(s32[1,7]{1,0:T(1,128)} %param.14) | copy-start | bytes 88
  7.2 46.0 %copy-start.2 = (f32[1,512,128]{2,1,0:T(8,128)S(1)}, f32[1,512,128]{2,1,0:T(8,128)}, u32[]{:S(2)}) copy-start(f32[1,512,128]{2,1,0:T(8,128)} %param.10) | copy-start | bytes 786436
  7.2 62.8 %reduce-scatter.3.cloned.1.call-start = ((), (), s32[]{:S(2)}) async-start(), calls=%async_computation.2 | async-start | bytes 163840 | tf_op jit(solution)/shard_map/reduce_scatter | solution.py:81
  8.3 45.0 %collective-permute-start = (bf16[1,512,128]{2,1,0:T(8,128)(2,1)S(1)}, bf16[1,512,128]{2,1,0:T(8,128)(2,1)S(1)}, u32[]{:S(2)}, u32[]{:S(2)}) collective-permute-start(bf16[1,512,128]{2,1,0:T(8,128)(2,1)S(1)} %convert_element_type.34), channel_id=1, source_target_pairs={{0,4},{1,5},{2,6},{3,7},{4,8},{5,9},{6,10},{7,11},{8,12},{9,13},{1... | collective-permute-start | bytes 393224 | tf_op jit(solution)/shard_map/ppermute | solution.py:16
  11.4 42.6 %collective-permute-start.1 = (bf16[1,512,128]{2,1,0:T(8,128)(2,1)S(1)}, bf16[1,512,128]{2,1,0:T(8,128)(2,1)S(1)}, u32[]{:S(2)}, u32[]{:S(2)}) collective-permute-start(bf16[1,512,128]{2,1,0:T(8,128)(2,1)S(1)} %convert_element_type.34), channel_id=1, source_target_pairs={{0,3},{1,4},{2,5},{3,6},{4,7},{5,8},{6,9},{7,10},{8,11},{9,12},{10... | collective-permute-start | bytes 393224 | tf_op jit(solution)/shard_map/ppermute | solution.py:16
  12.1 42.0 %collective-permute-start.2 = (bf16[1,512,128]{2,1,0:T(8,128)(2,1)S(1)}, bf16[1,512,128]{2,1,0:T(8,128)(2,1)S(1)}, u32[]{:S(2)}, u32[]{:S(2)}) collective-permute-start(bf16[1,512,128]{2,1,0:T(8,128)(2,1)S(1)} %convert_element_type.34), channel_id=1, source_target_pairs={{0,2},{1,3},{2,4},{3,5},{4,6},{5,7},{6,8},{7,9},{8,10},{9,11},{10,... | collective-permute-start | bytes 393224 | tf_op jit(solution)/shard_map/ppermute | solution.py:16
  13.6 41.1 %collective-permute-start.3 = (bf16[1,512,128]{2,1,0:T(8,128)(2,1)S(1)}, bf16[1,512,128]{2,1,0:T(8,128)(2,1)S(1)}, u32[]{:S(2)}, u32[]{:S(2)}) collective-permute-start(bf16[1,512,128]{2,1,0:T(8,128)(2,1)S(1)} %convert_element_type.34), channel_id=1, source_target_pairs={{0,1},{1,2},{2,3},{3,4},{4,5},{5,6},{6,7},{7,8},{8,9},{9,10},{10,1... | collective-permute-start | bytes 393224 | tf_op jit(solution)/shard_map/ppermute | solution.py:16
  14.3 40.5 %collective-permute-start.4 = (bf16[1,512,128]{2,1,0:T(8,128)(2,1)S(1)}, bf16[1,512,128]{2,1,0:T(8,128)(2,1)S(1)}, u32[]{:S(2)}, u32[]{:S(2)}) collective-permute-start(bf16[1,512,128]{2,1,0:T(8,128)(2,1)S(1)} %convert_element_type.34), channel_id=1, source_target_pairs={{0,31},{1,0},{2,1},{3,2},{4,3},{5,4},{6,5},{7,6},{8,7},{9,8},{10,9... | collective-permute-start | bytes 393224 | tf_op jit(solution)/shard_map/ppermute | solution.py:16
  52.9 75.5 %reduce-scatter.5.cloned.1.call-start = ((), (), s32[]{:S(2)}) async-start(), calls=%async_computation.3 | async-start | bytes 163840 | tf_op jit(solution)/shard_map/reduce_scatter | solution.py:81
  53.3 6.3 %collective-permute-start.5 = (bf16[1,512,128]{2,1,0:T(8,128)(2,1)S(1)}, bf16[1,512,128]{2,1,0:T(8,128)(2,1)S(1)}, u32[]{:S(2)}, u32[]{:S(2)}) collective-permute-start(bf16[1,512,128]{2,1,0:T(8,128)(2,1)S(1)} %convert_element_type.34), channel_id=1, source_target_pairs={{0,30},{1,31},{2,0},{3,1},{4,2},{5,3},{6,4},{7,5},{8,6},{9,7},{10,... | collective-permute-start | bytes 393224 | tf_op jit(solution)/shard_map/ppermute | solution.py:16
  54.0 6.0 %collective-permute-start.6 = (bf16[1,512,128]{2,1,0:T(8,128)(2,1)S(1)}, bf16[1,512,128]{2,1,0:T(8,128)(2,1)S(1)}, u32[]{:S(2)}, u32[]{:S(2)}) collective-permute-start(bf16[1,512,128]{2,1,0:T(8,128)(2,1)S(1)} %convert_element_type.34), channel_id=1, source_target_pairs={{0,29},{1,30},{2,31},{3,0},{4,1},{5,2},{6,3},{7,4},{8,5},{9,6},{10... | collective-permute-start | bytes 393224 | tf_op jit(solution)/shard_map/ppermute | solution.py:16
  54.1 8.5 %collective-permute-start.7 = (bf16[1,512,128]{2,1,0:T(8,128)(2,1)S(1)}, bf16[1,512,128]{2,1,0:T(8,128)(2,1)S(1)}, u32[]{:S(2)}, u32[]{:S(2)}) collective-permute-start(bf16[1,512,128]{2,1,0:T(8,128)(2,1)S(1)} %convert_element_type.34), channel_id=1, source_target_pairs={{0,28},{1,29},{2,30},{3,31},{4,0},{5,1},{6,2},{7,3},{8,4},{9,5},{1... | collective-permute-start | bytes 393224 | tf_op jit(solution)/shard_map/ppermute | solution.py:16
  59.6 3.7 %copy-start.6 = (f32[1,7]{1,0:T(1,128)S(1)}, f32[1,7]{1,0:T(1,128)}, u32[]{:S(2)}) copy-start(f32[1,7]{1,0:T(1,128)} %param.13) | copy-start | bytes 88
  66.8 12.6 %copy-start.3 = (bf16[1,512,64]{1,2,0:T(8,128)(2,1)S(1)}, bf16[1,512,64]{1,2,0:T(8,128)(2,1)}, u32[]{:S(2)}) copy-start(bf16[1,512,64]{1,2,0:T(8,128)(2,1)} %param.15) | copy-start | bytes 196612
  66.8 43.6 %copy-start.5 = (bf16[4,8,64,64]{3,2,1,0:T(8,128)(2,1)S(1)}, bf16[4,8,64,64]{3,2,1,0:T(8,128)(2,1)}, u32[]{:S(2)}) copy-start(bf16[4,8,64,64]{3,2,1,0:T(8,128)(2,1)} %param.17) | copy-start | bytes 786436
  71.0 40.5 %collective-permute-start.8 = (bf16[1,512,128]{1,2,0:T(8,128)(2,1)S(1)}, bf16[1,512,128]{1,2,0:T(8,128)(2,1)S(1)}, u32[]{:S(2)}, u32[]{:S(2)}) collective-permute-start(bf16[1,512,128]{1,2,0:T(8,128)(2,1)S(1)} %get-tuple-element.7), channel_id=1, source_target_pairs={{0,4},{1,5},{2,6},{3,7},{4,8},{5,9},{6,10},{7,11},{8,12},{9,13},{1... | collective-permute-start | bytes 393224 | tf_op jit(solution)/shard_map/ppermute | solution.py:16
  72.5 39.5 %collective-permute-start.9 = (bf16[1,512,128]{1,2,0:T(8,128)(2,1)S(1)}, bf16[1,512,128]{1,2,0:T(8,128)(2,1)S(1)}, u32[]{:S(2)}, u32[]{:S(2)}) collective-permute-start(bf16[1,512,128]{1,2,0:T(8,128)(2,1)S(1)} %get-tuple-element.7), channel_id=1, source_target_pairs={{0,3},{1,4},{2,5},{3,6},{4,7},{5,8},{6,9},{7,10},{8,11},{9,12},{10... | collective-permute-start | bytes 393224 | tf_op jit(solution)/shard_map/ppermute | solution.py:16
  72.5 39.6 %collective-permute-start.10 = (bf16[1,512,128]{1,2,0:T(8,128)(2,1)S(1)}, bf16[1,512,128]{1,2,0:T(8,128)(2,1)S(1)}, u32[]{:S(2)}, u32[]{:S(2)}) collective-permute-start(bf16[1,512,128]{1,2,0:T(8,128)(2,1)S(1)} %get-tuple-element.7), channel_id=1, source_target_pairs={{0,2},{1,3},{2,4},{3,5},{4,6},{5,7},{6,8},{7,9},{8,10},{9,11},{10,... | collective-permute-start | bytes 393224 | tf_op jit(solution)/shard_map/ppermute | solution.py:16
  74.1 39.0 %collective-permute-start.11 = (bf16[1,512,128]{1,2,0:T(8,128)(2,1)S(1)}, bf16[1,512,128]{1,2,0:T(8,128)(2,1)S(1)}, u32[]{:S(2)}, u32[]{:S(2)}) collective-permute-start(bf16[1,512,128]{1,2,0:T(8,128)(2,1)S(1)} %get-tuple-element.7), channel_id=1, source_target_pairs={{0,1},{1,2},{2,3},{3,4},{4,5},{5,6},{6,7},{7,8},{8,9},{9,10},{10,1... | collective-permute-start | bytes 393224 | tf_op jit(solution)/shard_map/ppermute | solution.py:16
  74.4 38.7 %collective-permute-start.12 = (bf16[1,512,128]{1,2,0:T(8,128)(2,1)S(1)}, bf16[1,512,128]{1,2,0:T(8,128)(2,1)S(1)}, u32[]{:S(2)}, u32[]{:S(2)}) collective-permute-start(bf16[1,512,128]{1,2,0:T(8,128)(2,1)S(1)} %get-tuple-element.7), channel_id=1, source_target_pairs={{0,31},{1,0},{2,1},{3,2},{4,3},{5,4},{6,5},{7,6},{8,7},{9,8},{10,9... | collective-permute-start | bytes 393224 | tf_op jit(solution)/shard_map/ppermute | solution.py:16
  111.4 6.4 %collective-permute-start.13 = (bf16[1,512,128]{1,2,0:T(8,128)(2,1)S(1)}, bf16[1,512,128]{1,2,0:T(8,128)(2,1)S(1)}, u32[]{:S(2)}, u32[]{:S(2)}) collective-permute-start(bf16[1,512,128]{1,2,0:T(8,128)(2,1)S(1)} %get-tuple-element.7), channel_id=1, source_target_pairs={{0,30},{1,31},{2,0},{3,1},{4,2},{5,3},{6,4},{7,5},{8,6},{9,7},{10,... | collective-permute-start | bytes 393224 | tf_op jit(solution)/shard_map/ppermute | solution.py:16
  112.0 5.9 %collective-permute-start.14 = (bf16[1,512,128]{1,2,0:T(8,128)(2,1)S(1)}, bf16[1,512,128]{1,2,0:T(8,128)(2,1)S(1)}, u32[]{:S(2)}, u32[]{:S(2)}) collective-permute-start(bf16[1,512,128]{1,2,0:T(8,128)(2,1)S(1)} %get-tuple-element.7), channel_id=1, source_target_pairs={{0,29},{1,30},{2,31},{3,0},{4,1},{5,2},{6,3},{7,4},{8,5},{9,6},{10... | collective-permute-start | bytes 393224 | tf_op jit(solution)/shard_map/ppermute | solution.py:16
  112.1 9.0 %collective-permute-start.15 = (bf16[1,512,128]{1,2,0:T(8,128)(2,1)S(1)}, bf16[1,512,128]{1,2,0:T(8,128)(2,1)S(1)}, u32[]{:S(2)}, u32[]{:S(2)}) collective-permute-start(bf16[1,512,128]{1,2,0:T(8,128)(2,1)S(1)} %get-tuple-element.7), channel_id=1, source_target_pairs={{0,28},{1,29},{2,30},{3,31},{4,0},{5,1},{6,2},{7,3},{8,4},{9,5},{1... | collective-permute-start | bytes 393224 | tf_op jit(solution)/shard_map/ppermute | solution.py:16
Sparse Core Ops, SparseCore 0:
  53.0 16.8 reduce-scatter.2
  111.6 16.8 reduce-scatter.4
where the time goes:
time: 138 us
  blocking collectives  61.6 us (45%)
  waiting for transfers between devices  22.1 us (16%)
  starting transfers between devices  22 us (16%)
  between operations  14.4 us (10%)
  matrix products  13 us (9%)
  local copies, waits for them, and re-layouts  3.54 us (3%)
    all_gather x2, blocking collectives, shards(): lax.all_gather(expansion_coefficients, ('near', 'row'), axis=0, tiled=True)  61.6 us
    ppermute x16, starting transfers between devices, shifted(): return lax.ppermute(value, axis, pairs)  21.9 us
    ppermute x16, waiting for transfers between devices, shifted(): return lax.ppermute(value, axis, pairs)  15.7 us
    dot_general x2, matrix products, shards(): jnp.einsum('ijkl,ijlc->ijkc', near_tiles, nearby, preferred_element_type=...  6.86 us
    reduce_scatter x2, waiting for transfers between devices, shards(): lax.psum_scatter(partial_coefs, 'col', scatter_dimension=0, tiled=True)  6.38 us
    dot_general x2, matrix products, shards(): jnp.einsum('lqsx,qxp->lsp', masked_values, lax.all_gather(expansion_coeff...  3.06 us
  transfers between devices with their start and end apart: 18, of which 7 were waited for; matrix products, arithmetic and copies ran while one was open for 9% of the time, Pallas kernels for 0%

commit v1 on v0

v1 whole, which is shorter than its diff:
```python
import functools

import jax
import jax.numpy as jnp
from jax import lax
from jax.experimental import pallas as pl
from jax.experimental.pallas import tpu as pltpu
from jax.sharding import PartitionSpec as P

REACH = 4
ITERS = 2
DAMPING = 0.5
AXES = ("near", "row", "col")
MESH = pl.DeviceIdType.MESH


def kernel(
    sizes,
    neighbours,
    scales,
    right_hbm,
    guess_hbm,
    tiles_hbm,
    source_hbm,
    basis_hbm,
    couplings_hbm,
    x_out,
    residual_out,
    right,
    iterate,
    tiles,
    source,
    basis,
    couplings,
    masked,
    total,
    window,
    coefs,
    parts_out,
    parts_in,
    load_sems,
    halo_send,
    halo_recv,
    coef_send,
    coef_recv,
    part_send,
    part_recv,
):
    n_near, n_row, n_col = sizes
    groups = n_near * n_row
    clusters = groups * n_col
    near, row, col = (lax.axis_index(a) for a in AXES)
    group = near * n_row + row
    me = group * n_col + col
    slots = 2 * REACH + 1
    rank = coefs.shape[2]
    listed = neighbours.shape[1]

    def place(device):
        return (device // (n_row * n_col), device // n_col % n_row, device % n_col)

    def shifted(d):
        return place((me + d + clusters) % clusters)

    def group_peer(i):
        return place((group + i) % groups * n_col + col)

    def col_peer(i):
        return (near, row, (col + i) % n_col)

    loads = [
        pltpu.make_async_copy(src.at[0] if lead else src, dst, load_sems.at[i])
        for i, (src, dst, lead) in enumerate(
            (
                (guess_hbm, iterate, True),
                (source_hbm, source, True),
                (couplings_hbm, couplings, False),
                (tiles_hbm, tiles, True),
                (basis_hbm, basis, True),
                (right_hbm, right, True),
            )
        )
    ]
    for load in loads:
        load.start()

    order = [d for step in range(1, REACH + 1) for d in (step, -step)]
    barrier = pltpu.get_barrier_semaphore()
    for d in order:
        pl.semaphore_signal(barrier, inc=1, device_id=shifted(d), device_id_type=MESH)

    def greet(i, carry):
        pl.semaphore_signal(barrier, inc=1, device_id=group_peer(i), device_id_type=MESH)
        return carry

    lax.fori_loop(1, groups, greet, 0)
    for i in range(1, n_col):
        pl.semaphore_signal(barrier, inc=1, device_id=col_peer(i), device_id_type=MESH)

    choice, weight = [], []
    for j in range(slots):
        pick, scale = jnp.int32(0), jnp.float32(0.0)
        for k in range(listed):
            hit = (neighbours[0, k] - me + REACH + clusters) % clusters == j
            pick = jnp.where(hit, jnp.int32(k), pick)
            scale = jnp.where(hit, scales[0, k], scale)
        choice.append(pick)
        weight.append(scale)

    def coef_copy(sweep, i):
        return pltpu.make_async_remote_copy(
            src_ref=coefs.at[sweep, group],
            dst_ref=coefs.at[sweep, group],
            send_sem=coef_send.at[sweep],
            recv_sem=coef_recv.at[sweep],
            device_id=group_peer(i),
            device_id_type=MESH,
        )

    def halo_copy(sweep, d):
        return pltpu.make_async_remote_copy(
            src_ref=window.at[sweep, REACH],
            dst_ref=window.at[sweep, REACH - d],
            send_sem=halo_send.at[sweep, REACH + d],
            recv_sem=halo_recv.at[sweep, REACH - d],
            device_id=shifted(d),
            device_id_type=MESH,
        )

    def part_copy(sweep, i):
        return pltpu.make_async_remote_copy(
            src_ref=parts_out.at[sweep, i],
            dst_ref=parts_in.at[sweep, i],
            send_sem=part_send.at[sweep, i],
            recv_sem=part_recv.at[sweep, i],
            device_id=col_peer(i),
            device_id_type=MESH,
        )

    def near_product(sweep, j):
        return weight[j] * jnp.dot(
            tiles[choice[j]], window[sweep, j], preferred_element_type=jnp.float32
        )

    loads[0].wait()
    loads[1].wait()
    for sweep in range(ITERS):
        coarse = iterate[...].astype(jnp.bfloat16)
        window[sweep, REACH] = coarse
        coefs[sweep, group] = lax.dot_general(
            source[...], coarse, (((0,), (0,)), ((), ())), preferred_element_type=jnp.float32
        ).astype(jnp.bfloat16)
        if sweep == 0:
            pl.semaphore_wait(barrier, len(order) + groups - 1 + n_col - 1)

        def send(i, carry):
            coef_copy(sweep, i).start()
            return carry

        lax.fori_loop(1, groups, send, 0)
        for d in order:
            halo_copy(sweep, d).start()

        if sweep == 0:
            loads[2].wait()
            for q in range(0, groups, 2):
                sides = []
                for p in (q, q + 1):
                    rows = []
                    for l in range(n_col):
                        distance = (group * n_col + l - (p * n_col + col) + clusters) % clusters
                        far = jnp.minimum(distance, clusters - distance) > REACH
                        rows.append(couplings[l, p].astype(jnp.float32) * far.astype(jnp.float32))
                    sides.append(jnp.concatenate(rows, axis=0).astype(jnp.bfloat16))
                masked[:, q * rank : (q + 2) * rank] = jnp.concatenate(sides, axis=1)
            for load in loads[3:]:
                load.wait()

        total[...] = iterate[...] + near_product(sweep, REACH)

        pltpu.make_async_copy(
            coefs.at[sweep, pl.ds(0, groups - 1)],
            coefs.at[sweep, pl.ds(0, groups - 1)],
            coef_recv.at[sweep],
        ).wait()
        partial = jnp.dot(
            masked[...],
            coefs[sweep].reshape(groups * rank, -1),
            preferred_element_type=jnp.float32,
        ).reshape(n_col, rank, -1)
        for l in range(n_col):
            parts_out[sweep, (l - col + n_col) % n_col] = partial[l].astype(jnp.bfloat16)
        for i in range(1, n_col):
            part_copy(sweep, i).start()

        for d in order[: len(order) // 2]:
            halo_copy(sweep, -d).wait_recv()
            total[...] += near_product(sweep, REACH + d)

        far_coefs = parts_out[sweep, 0].astype(jnp.float32)
        for i in range(1, n_col):
            part_copy(sweep, i).wait_recv()
            far_coefs += parts_in[sweep, i].astype(jnp.float32)
        total[...] += jnp.dot(
            basis[...], far_coefs.astype(jnp.bfloat16), preferred_element_type=jnp.float32
        )

        for d in order[len(order) // 2 :]:
            halo_copy(sweep, -d).wait_recv()
            total[...] += near_product(sweep, REACH + d)

        residual = right[...] - total[...]
        if sweep == ITERS - 1:
            residual_out[0] = residual
            x_out[0] = iterate[...] + DAMPING * residual
        else:
            iterate[...] = iterate[...] + DAMPING * residual

    for sweep in range(ITERS):
        pltpu.make_async_copy(
            coefs.at[sweep, pl.ds(0, groups - 1)],
            coefs.at[sweep, pl.ds(0, groups - 1)],
            coef_send.at[sweep],
        ).wait()
        for d in order:
            halo_copy(sweep, d).wait_send()
        for i in range(1, n_col):
            part_copy(sweep, i).wait_send()


def shards(
    sizes,
    right_side,
    start_guess,
    near_tiles,
    tile_scales,
    neighbours,
    source_cluster_basis,
    basis_out,
    couplings,
):
    local_count, leaf, rhs = right_side.shape
    targets, groups, rank, _ = couplings.shape
    assert local_count == 1 and targets == sizes[2]
    listed = near_tiles.shape[1]
    any_spec = pl.BlockSpec(memory_space=pl.ANY)
    small = pl.BlockSpec(memory_space=pltpu.SMEM)
    vmem = pl.BlockSpec(memory_space=pltpu.VMEM)
    slots = 2 * REACH + 1
    bf16, f32 = jnp.bfloat16, jnp.float32
    dma = pltpu.SemaphoreType.DMA
    return pl.pallas_call(
        functools.partial(kernel, sizes),
        out_shape=[jax.ShapeDtypeStruct(right_side.shape, f32)] * 2,
        in_specs=[small] * 2 + [any_spec] * 6,
        out_specs=[vmem] * 2,
        scratch_shapes=[
            pltpu.VMEM((leaf, rhs), f32),
            pltpu.VMEM((leaf, rhs), f32),
            pltpu.VMEM((listed, leaf, leaf), bf16),
            pltpu.VMEM((leaf, rank), bf16),
            pltpu.VMEM((leaf, rank), bf16),
            pltpu.VMEM(couplings.shape, bf16),
            pltpu.VMEM((targets * rank, groups * rank), bf16),
            pltpu.VMEM((leaf, rhs), f32),
            pltpu.VMEM((ITERS, slots, leaf, rhs), bf16),
            pltpu.VMEM((ITERS, groups, rank, rhs), bf16),
            pltpu.VMEM((ITERS, targets, rank, rhs), bf16),
            pltpu.VMEM((ITERS, targets, rank, rhs), bf16),
            dma((6,)),
            dma((ITERS, slots)),
            dma((ITERS, slots)),
            dma((ITERS,)),
            dma((ITERS,)),
            dma((ITERS, targets)),
            dma((ITERS, targets)),
        ],
        compiler_params=pltpu.CompilerParams(collective_id=0, has_side_effects=True),
    )(
        neighbours,
        tile_scales,
        right_side,
        start_guess,
        near_tiles,
        source_cluster_basis,
        basis_out,
        couplings,
    )


def solution(mesh):
    sizes = tuple(mesh.shape[a] for a in AXES)
    lead = P(AXES, None, None)
    in_specs = (
        lead,
        lead,
        P(AXES, None, None, None),
        P(AXES, None),
        P(AXES, None),
        lead,
        lead,
        P(("near", "row"), "col", None, None),
    )
    body = functools.partial(shards, sizes)
    return jax.shard_map(
        body, mesh=mesh, in_specs=in_specs, out_specs=(lead, lead), check_vma=False
    )
```

time: 138 us -> 54.8 us (0.40)
  blocking collectives: 61.6 us -> 0 us
  Pallas kernels: 0 us -> 47.3 us
  waiting for transfers between devices: 22.1 us -> 0 us
  starting transfers between devices: 22 us -> 0 us
  between operations: 14.4 us -> 0.64 us
  matrix products: 13 us -> 0 us
  local copies, waits for them, and re-layouts: 3.54 us -> 6.54 us
    all_gather x2 -> x0, blocking collectives: 61.6 us -> none  [shards(): lax.all_gather(expansion_coefficients, ('near', 'row'), axis=0, tiled=True)]
    pallas_call x0 -> x1, Pallas kernels: none -> 47.3 us  [shards(): pl.pallas_call(functools.partial(kernel, sizes), out_shape=[jax.ShapeDtyp...]
    ppermute x16 -> x0, starting transfers between devices: 21.9 us -> none  [shifted(): return lax.ppermute(value, axis, pairs)]
    ppermute x16 -> x0, waiting for transfers between devices: 15.7 us -> none  [shifted(): return lax.ppermute(value, axis, pairs)]
    dot_general x8 -> x0, matrix products: 13 us -> none  [the longest x2 6.86 us: shards(): jnp.einsum('ijkl,ijlc->ijkc', near_tiles, nearby, preferred_element_type=...]
    reduce_scatter x2 -> x0, waiting for transfers between devices: 6.38 us -> none  [shards(): lax.psum_scatter(partial_coefs, 'col', scatter_dimension=0, tiled=True)]
    unnamed x33 -> x4, local copies, waits for them, and re-layouts: 2.18 us -> 6.54 us
  transfers between devices with their start and end apart: 18 -> 0, of which waited for: 7 -> 0; matrix products, arithmetic and copies ran while one was open for 9% -> 0% of each run, Pallas kernels for 0% -> 0%
where the time goes in v1:
time: 54.8 us; the launch traced here: 54.5 us
  Pallas kernels  47.3 us (86%)
  local copies, waits for them, and re-layouts  6.54 us (12%)
  between operations  0.64 us (1%)
    pallas_call x1, Pallas kernels, shards(): pl.pallas_call(functools.partial(kernel, sizes), out_shape=[jax.ShapeDtyp...  47.3 us
    unnamed x4, local copies, waits for them, and re-layouts  6.54 us

profile of v1, /device:TPU:0, one launch (start us, length us, event | category | flops | bytes accessed | tf_op | source)
XLA Modules:
  0.0 54.5 jit_solution(10531132196845432146)
XLA Ops:
  0.6 1.6 %copy.10.source_hbm = bf16[1,512,64]{2,1,0:T(8,128)(2,1)} copy(bf16[1,512,64]{1,2,0:T(8,128)(2,1)} %param.13) | data formatting | bytes 131072 | tf_op args[5]
  2.2 1.6 %copy.11.basis_hbm = bf16[1,512,64]{2,1,0:T(8,128)(2,1)} copy(bf16[1,512,64]{1,2,0:T(8,128)(2,1)} %param.14) | data formatting | bytes 131072 | tf_op args[6]
  3.8 47.3 %shard_map.95 = (f32[1,512,128]{2,1,0:T(8,128)}, f32[1,512,128]{2,1,0:T(8,128)}) custom-call(s32[1,7]{1,0:T(1,128)} %neighbours.1, f32[1,7]{1,0:T(1,128)} %scales.1, f32[1,512,128]{2,1,0:T(8,128)} %right_hbm.1, f32[1,512,128]{2,1,0:T(8,128)} %guess_hbm.1, bf16[1,7,512,512]{3,2,1,0:T(8,128)(2,1)} %tiles_hbm.1, bf16[1,512,64]{2,1,0:T(8,128)(2,1)} %copy.10.source_hbm, ...), custom_call_target="tpu_custom_call" | custom-call | tf_op jit(solution)/shard_map/pallas_call | solution.py:252
  51.2 1.7 %copy.14 = f32[1,512,128]{2,1,0:T(8,128)} copy(f32[1,512,128]{2,1,0:T(8,128)} %get-tuple-element.4) | data formatting | bytes 524288
  52.8 1.7 %copy.15 = f32[1,512,128]{2,1,0:T(8,128)} copy(f32[1,512,128]{2,1,0:T(8,128)} %get-tuple-element.5) | data formatting | bytes 524288

commit v2 on v1

--- a/solution.py
+++ b/solution.py
@@ -24,8 +24,8 @@
     source_hbm,
     basis_hbm,
     couplings_hbm,
-    x_out,
-    residual_out,
+    last,
+    applied,
     right,
     iterate,
     tiles,
@@ -59,9 +59,6 @@
     def place(device):
         return (device // (n_row * n_col), device // n_col % n_row, device % n_col)
 
-    def shifted(d):
-        return place((me + d + clusters) % clusters)
-
     def group_peer(i):
         return place((group + i) % groups * n_col + col)
 
@@ -84,11 +81,7 @@
     for load in loads:
         load.start()
 
-    order = [d for step in range(1, REACH + 1) for d in (step, -step)]
     barrier = pltpu.get_barrier_semaphore()
-    for d in order:
-        pl.semaphore_signal(barrier, inc=1, device_id=shifted(d), device_id_type=MESH)
-
     def greet(i, carry):
         pl.semaphore_signal(barrier, inc=1, device_id=group_peer(i), device_id_type=MESH)
         return carry
@@ -97,15 +90,15 @@
     for i in range(1, n_col):
         pl.semaphore_signal(barrier, inc=1, device_id=col_peer(i), device_id_type=MESH)
 
-    choice, weight = [], []
-    for j in range(slots):
-        pick, scale = jnp.int32(0), jnp.float32(0.0)
-        for k in range(listed):
-            hit = (neighbours[0, k] - me + REACH + clusters) % clusters == j
-            pick = jnp.where(hit, jnp.int32(k), pick)
-            scale = jnp.where(hit, scales[0, k], scale)
-        choice.append(pick)
-        weight.append(scale)
+    offsets = [
+        (neighbours[0, k] - me + REACH + clusters) % clusters - REACH for k in range(listed)
+    ]
+    side = 1 - col // (n_col // 2) * 2
+    parity = col % 2 * 2 - 1
+    ahead = place((me + n_col) % clusters)
+    behind = place((me + clusters - n_col) % clusters)
+    across = place(me + 2 * side)
+    partner = place(me - parity)
 
     def coef_copy(sweep, i):
         return pltpu.make_async_remote_copy(
@@ -117,15 +110,20 @@
             device_id_type=MESH,
         )
 
-    def halo_copy(sweep, d):
+    def halo_copy(sweep, number, block, target, lands):
         return pltpu.make_async_remote_copy(
-            src_ref=window.at[sweep, REACH],
-            dst_ref=window.at[sweep, REACH - d],
-            send_sem=halo_send.at[sweep, REACH + d],
-            recv_sem=halo_recv.at[sweep, REACH - d],
-            device_id=shifted(d),
+            src_ref=window.at[sweep, REACH + block],
+            dst_ref=window.at[sweep, REACH + lands],
+            send_sem=halo_send.at[sweep, number],
+            recv_sem=halo_recv.at[sweep, REACH + lands],
+            device_id=target,
             device_id_type=MESH,
         )
+
+    def halo_wait(sweep, d):
+        pltpu.make_async_copy(
+            window.at[sweep, REACH + d], window.at[sweep, REACH + d], halo_recv.at[sweep, REACH + d]
+        ).wait()
 
     def part_copy(sweep, i):
         return pltpu.make_async_remote_copy(
@@ -137,10 +135,30 @@
             device_id_type=MESH,
         )
 
-    def near_product(sweep, j):
-        return weight[j] * jnp.dot(
-            tiles[choice[j]], window[sweep, j], preferred_element_type=jnp.float32
-        )
+    def near_product(sweep, d):
+        pick, scale = jnp.int32(0), jnp.float32(0.0)
+        for k in range(listed):
+            hit = offsets[k] == d
+            pick = jnp.where(hit, jnp.int32(k), pick)
+            scale = jnp.where(hit, scales[0, k], scale)
+        return scale * jnp.dot(
+            tiles[pick], window[sweep, REACH + d], preferred_element_type=jnp.float32
+        )
+
+    def add_near(sweep, d):
+        total[...] += near_product(sweep, d)
+
+    def copies(sweep):
+        return [
+            halo_copy(sweep, 0, 0, ahead, -n_col),
+            halo_copy(sweep, 1, 0, behind, n_col),
+            halo_copy(sweep, 2, 0, across, -2 * side),
+            halo_copy(sweep, 3, 0, partner, parity),
+            halo_copy(sweep, 4, n_col * side, across, 2 * side),
+            halo_copy(sweep, 5, 2 * side, partner, 2 * side + parity),
+            halo_copy(sweep, 6, -n_col * parity, partner, -3 * parity),
+            halo_copy(sweep, 7, -2 * side, partner, -2 * side + parity),
+        ]
 
     loads[0].wait()
     loads[1].wait()
@@ -148,18 +166,19 @@
         coarse = iterate[...].astype(jnp.bfloat16)
         window[sweep, REACH] = coarse
         coefs[sweep, group] = lax.dot_general(
-            source[...], coarse, (((0,), (0,)), ((), ())), preferred_element_type=jnp.float32
+            source[...], coarse, (((1,), (0,)), ((), ())), preferred_element_type=jnp.float32
         ).astype(jnp.bfloat16)
         if sweep == 0:
-            pl.semaphore_wait(barrier, len(order) + groups - 1 + n_col - 1)
+            pl.semaphore_wait(barrier, groups - 1 + n_col - 1)
 
         def send(i, carry):
             coef_copy(sweep, i).start()
             return carry
 
         lax.fori_loop(1, groups, send, 0)
-        for d in order:
-            halo_copy(sweep, d).start()
+        halo = copies(sweep)
+        for copy in halo[:4]:
+            copy.start()
 
         if sweep == 0:
             loads[2].wait()
@@ -176,7 +195,12 @@
             for load in loads[3:]:
                 load.wait()
 
-        total[...] = iterate[...] + near_product(sweep, REACH)
+        total[...] = iterate[...] + near_product(sweep, 0)
+        halo_wait(sweep, 2 * side)
+        halo[5].start()
+        add_near(sweep, 2 * side)
+        halo_wait(sweep, -parity)
+        add_near(sweep, -parity)
 
         pltpu.make_async_copy(
             coefs.at[sweep, pl.ds(0, groups - 1)],
@@ -193,28 +217,47 @@
         for i in range(1, n_col):
             part_copy(sweep, i).start()
 
-        for d in order[: len(order) // 2]:
-            halo_copy(sweep, -d).wait_recv()
-            total[...] += near_product(sweep, REACH + d)
+        halo_wait(sweep, n_col * side)
+        halo[4].start()
+
+        @pl.when(parity == -side)
+        def _():
+            halo[6].start()
+
+        add_near(sweep, n_col * side)
+        halo_wait(sweep, -n_col * side)
+
+        @pl.when(parity == side)
+        def _():
+            halo[6].start()
+
+        add_near(sweep, -n_col * side)
+        halo_wait(sweep, 2 * side - parity)
+        add_near(sweep, 2 * side - parity)
 
         far_coefs = parts_out[sweep, 0].astype(jnp.float32)
         for i in range(1, n_col):
             part_copy(sweep, i).wait_recv()
             far_coefs += parts_in[sweep, i].astype(jnp.float32)
-        total[...] += jnp.dot(
-            basis[...], far_coefs.astype(jnp.bfloat16), preferred_element_type=jnp.float32
-        )
-
-        for d in order[len(order) // 2 :]:
-            halo_copy(sweep, -d).wait_recv()
-            total[...] += near_product(sweep, REACH + d)
-
-        residual = right[...] - total[...]
+        total[...] += lax.dot_general(
+            basis[...],
+            far_coefs.astype(jnp.bfloat16),
+            (((0,), (0,)), ((), ())),
+            preferred_element_type=jnp.float32,
+        )
+
+        halo_wait(sweep, -2 * side)
+        halo[7].start()
+        add_near(sweep, -2 * side)
+        for d in (3 * parity, -2 * side - parity):
+            halo_wait(sweep, d)
+            add_near(sweep, d)
+
         if sweep == ITERS - 1:
-            residual_out[0] = residual
-            x_out[0] = iterate[...] + DAMPING * residual
+            applied[0] = total[...]
+            last[0] = iterate[...]
         else:
-            iterate[...] = iterate[...] + DAMPING * residual
+            iterate[...] = iterate[...] + DAMPING * (right[...] - total[...])
 
     for sweep in range(ITERS):
         pltpu.make_async_copy(
@@ -222,8 +265,8 @@
             coefs.at[sweep, pl.ds(0, groups - 1)],
             coef_send.at[sweep],
         ).wait()
-        for d in order:
-            halo_copy(sweep, d).wait_send()
+        for copy in copies(sweep):
+            copy.wait_send()
         for i in range(1, n_col):
             part_copy(sweep, i).wait_send()
 
@@ -241,7 +284,7 @@
 ):
     local_count, leaf, rhs = right_side.shape
     targets, groups, rank, _ = couplings.shape
-    assert local_count == 1 and targets == sizes[2]
+    assert local_count == 1 and targets == sizes[2] == REACH
     listed = near_tiles.shape[1]
     any_spec = pl.BlockSpec(memory_space=pl.ANY)
     small = pl.BlockSpec(memory_space=pltpu.SMEM)
@@ -249,7 +292,7 @@
     slots = 2 * REACH + 1
     bf16, f32 = jnp.bfloat16, jnp.float32
     dma = pltpu.SemaphoreType.DMA
-    return pl.pallas_call(
+    last, applied = pl.pallas_call(
         functools.partial(kernel, sizes),
         out_shape=[jax.ShapeDtypeStruct(right_side.shape, f32)] * 2,
         in_specs=[small] * 2 + [any_spec] * 6,
@@ -258,8 +301,8 @@
             pltpu.VMEM((leaf, rhs), f32),
             pltpu.VMEM((leaf, rhs), f32),
             pltpu.VMEM((listed, leaf, leaf), bf16),
-            pltpu.VMEM((leaf, rank), bf16),
-            pltpu.VMEM((leaf, rank), bf16),
+            pltpu.VMEM((rank, leaf), bf16),
+            pltpu.VMEM((rank, leaf), bf16),
             pltpu.VMEM(couplings.shape, bf16),
             pltpu.VMEM((targets * rank, groups * rank), bf16),
             pltpu.VMEM((leaf, rhs), f32),
@@ -268,7 +311,7 @@
             pltpu.VMEM((ITERS, targets, rank, rhs), bf16),
             pltpu.VMEM((ITERS, targets, rank, rhs), bf16),
             dma((6,)),
-            dma((ITERS, slots)),
+            dma((ITERS, 8)),
             dma((ITERS, slots)),
             dma((ITERS,)),
             dma((ITERS,)),
@@ -282,10 +325,12 @@
         right_side,
         start_guess,
         near_tiles,
-        source_cluster_basis,
-        basis_out,
+        jnp.swapaxes(source_cluster_basis, 1, 2),
+        jnp.swapaxes(basis_out, 1, 2),
         couplings,
     )
+    residual = right_side - applied
+    return last + DAMPING * residual, residual
 
 
 def solution(mesh):

time: 54.8 us -> 41.3 us (0.75)
  Pallas kernels: 47.3 us -> 38.6 us
  local copies, waits for them, and re-layouts: 6.54 us -> 0.01 us
  other arithmetic: 0 us -> 1.86 us
    pallas_call x1, Pallas kernels: 47.3 us -> 38.6 us  [shards(): pl.pallas_call(functools.partial(kernel, sizes), out_shape=[jax.ShapeDtyp...]
    unnamed x4 -> x2, local copies, waits for them, and re-layouts: 6.54 us -> 0.01 us
    add x0 -> x1, other arithmetic: none -> 1.86 us  [shards(): return (last + DAMPING * residual, residual)]
where the time goes in v2:
time: 41.3 us; the launch traced here: 41.1 us
  Pallas kernels  38.6 us (93%)
  other arithmetic  1.86 us (5%)
  between operations  0.66 us (2%)
    pallas_call x1, Pallas kernels, shards(): pl.pallas_call(functools.partial(kernel, sizes), out_shape=[jax.ShapeDtyp...  38.6 us
    add x1, other arithmetic, shards(): return (last + DAMPING * residual, residual)  1.86 us

profile of v2, /device:TPU:0, one launch (start us, length us, event | category | flops | bytes accessed | tf_op | source)
XLA Modules:
  0.0 41.1 jit_solution(639944376553788997)
XLA Ops:
  0.6 0.0 copy-start
  0.6 38.6 %shard_map.95 = (f32[1,512,128]{2,1,0:T(8,128)}, f32[1,512,128]{2,1,0:T(8,128)}) custom-call(s32[1,7]{1,0:T(1,128)} %neighbours.1, f32[1,7]{1,0:T(1,128)} %scales.1, f32[1,512,128]{2,1,0:T(8,128)} %right_hbm.1, f32[1,512,128]{2,1,0:T(8,128)} %guess_hbm.1, bf16[1,7,512,512]{3,2,1,0:T(8,128)(2,1)} %tiles_hbm.1, bf16[1,64,512]{2,1,0:T(8,128)(2,1)} %bitcast.2, ...), custom_call_target="tpu_custom_call" | custom-call | tf_op jit(solution)/shard_map/pallas_call | solution.py:295
  39.2 0.0 copy-done
  39.3 1.9 %multiply_add_fusion = (f32[1,512,128]{2,1,0:T(8,128)}, f32[1,512,128]{2,1,0:T(8,128)}) fusion(f32[1,512,128]{2,1,0:T(8,128)} %get-tuple-element.4, f32[1,512,128]{2,1,0:T(8,128)S(1)} %copy-done, f32[1,512,128]{2,1,0:T(8,128)} %get-tuple-element.5), kind=kLoop, calls=%fused_computation | loop fusion | flops 196608 | bytes 1310720 | tf_op jit(solution)/shard_map/add | solution.py:333
Async XLA Ops:
  0.6 38.6 %copy-start = (f32[1,512,128]{2,1,0:T(8,128)S(1)}, f32[1,512,128]{2,1,0:T(8,128)}, u32[]{:S(2)}) copy-start(f32[1,512,128]{2,1,0:T(8,128)} %right_hbm.1) | copy-start | bytes 786436

commit v3 on v2

--- a/solution.py
+++ b/solution.py
@@ -9,6 +9,7 @@
 
 REACH = 4
 ITERS = 2
+CHUNKS = 4
 DAMPING = 0.5
 AXES = ("near", "row", "col")
 MESH = pl.DeviceIdType.MESH
@@ -100,30 +101,49 @@
     across = place(me + 2 * side)
     partner = place(me - parity)
 
-    def coef_copy(sweep, i):
+    def row_copy(sweep, i):
         return pltpu.make_async_remote_copy(
             src_ref=coefs.at[sweep, group],
             dst_ref=coefs.at[sweep, group],
-            send_sem=coef_send.at[sweep],
-            recv_sem=coef_recv.at[sweep],
-            device_id=group_peer(i),
+            send_sem=coef_send.at[sweep, 0],
+            recv_sem=coef_recv.at[sweep, 0],
+            device_id=(near, (row + i) % n_row, col),
             device_id_type=MESH,
         )
 
-    def halo_copy(sweep, number, block, target, lands):
+    def near_copy(sweep, i):
+        mine = pl.ds(near * n_row, n_row)
         return pltpu.make_async_remote_copy(
-            src_ref=window.at[sweep, REACH + block],
-            dst_ref=window.at[sweep, REACH + lands],
-            send_sem=halo_send.at[sweep, number],
-            recv_sem=halo_recv.at[sweep, REACH + lands],
+            src_ref=coefs.at[sweep, mine],
+            dst_ref=coefs.at[sweep, mine],
+            send_sem=coef_send.at[sweep, 1],
+            recv_sem=coef_recv.at[sweep, 1],
+            device_id=((near + i) % n_near, row, col),
+            device_id_type=MESH,
+        )
+
+    def coef_wait(sems, sweep, stage):
+        count = groups - n_row if stage else n_row - 1
+        part = coefs.at[sweep, pl.ds(0, count)]
+        pltpu.make_async_copy(part, part, sems.at[sweep, stage]).wait()
+
+    rows = window.shape[2] // CHUNKS
+
+    def halo_copy(sweep, number, block, target, lands, c):
+        span = pl.ds(c * rows, rows)
+        return pltpu.make_async_remote_copy(
+            src_ref=window.at[sweep, REACH + block, span],
+            dst_ref=window.at[sweep, REACH + lands, span],
+            send_sem=halo_send.at[sweep, number, c],
+            recv_sem=halo_recv.at[sweep, REACH + lands, c],
             device_id=target,
             device_id_type=MESH,
         )
 
-    def halo_wait(sweep, d):
-        pltpu.make_async_copy(
-            window.at[sweep, REACH + d], window.at[sweep, REACH + d], halo_recv.at[sweep, REACH + d]
-        ).wait()
+    def halo_wait(sweep, d, chunks=range(CHUNKS)):
+        for c in chunks:
+            piece = window.at[sweep, REACH + d, pl.ds(c * rows, rows)]
+            pltpu.make_async_copy(piece, piece, halo_recv.at[sweep, REACH + d, c]).wait()
 
     def part_copy(sweep, i):
         return pltpu.make_async_remote_copy(
@@ -148,17 +168,16 @@
     def add_near(sweep, d):
         total[...] += near_product(sweep, d)
 
-    def copies(sweep):
-        return [
-            halo_copy(sweep, 0, 0, ahead, -n_col),
-            halo_copy(sweep, 1, 0, behind, n_col),
-            halo_copy(sweep, 2, 0, across, -2 * side),
-            halo_copy(sweep, 3, 0, partner, parity),
-            halo_copy(sweep, 4, n_col * side, across, 2 * side),
-            halo_copy(sweep, 5, 2 * side, partner, 2 * side + parity),
-            halo_copy(sweep, 6, -n_col * parity, partner, -3 * parity),
-            halo_copy(sweep, 7, -2 * side, partner, -2 * side + parity),
-        ]
+    routes = [
+        (0, 0, ahead, -n_col),
+        (1, 0, behind, n_col),
+        (2, 0, across, -2 * side),
+        (3, 0, partner, parity),
+        (4, n_col * side, across, 2 * side),
+        (5, 2 * side, partner, 2 * side + parity),
+        (6, -n_col * parity, partner, -3 * parity),
+        (7, -2 * side, partner, -2 * side + parity),
+    ]
 
     loads[0].wait()
     loads[1].wait()
@@ -171,42 +190,43 @@
         if sweep == 0:
             pl.semaphore_wait(barrier, groups - 1 + n_col - 1)
 
-        def send(i, carry):
-            coef_copy(sweep, i).start()
-            return carry
-
-        lax.fori_loop(1, groups, send, 0)
-        halo = copies(sweep)
-        for copy in halo[:4]:
-            copy.start()
+        for i in range(1, n_row):
+            row_copy(sweep, i).start()
+        for c in range(CHUNKS):
+            for route in routes[:4]:
+                halo_copy(sweep, *route, c).start()
 
         if sweep == 0:
             loads[2].wait()
             for q in range(0, groups, 2):
                 sides = []
                 for p in (q, q + 1):
-                    rows = []
+                    stack = []
                     for l in range(n_col):
                         distance = (group * n_col + l - (p * n_col + col) + clusters) % clusters
                         far = jnp.minimum(distance, clusters - distance) > REACH
-                        rows.append(couplings[l, p].astype(jnp.float32) * far.astype(jnp.float32))
-                    sides.append(jnp.concatenate(rows, axis=0).astype(jnp.bfloat16))
+                        stack.append(couplings[l, p].astype(jnp.float32) * far.astype(jnp.float32))
+                    sides.append(jnp.concatenate(stack, axis=0).astype(jnp.bfloat16))
                 masked[:, q * rank : (q + 2) * rank] = jnp.concatenate(sides, axis=1)
             for load in loads[3:]:
                 load.wait()
 
         total[...] = iterate[...] + near_product(sweep, 0)
-        halo_wait(sweep, 2 * side)
-        halo[5].start()
-        add_near(sweep, 2 * side)
         halo_wait(sweep, -parity)
         add_near(sweep, -parity)
 
-        pltpu.make_async_copy(
-            coefs.at[sweep, pl.ds(0, groups - 1)],
-            coefs.at[sweep, pl.ds(0, groups - 1)],
-            coef_recv.at[sweep],
-        ).wait()
+        coef_wait(coef_recv, sweep, 0)
+
+        def pass_on(i, carry):
+            near_copy(sweep, i).start()
+            return carry
+
+        lax.fori_loop(1, n_near, pass_on, 0)
+        for c in range(CHUNKS):
+            halo_wait(sweep, 2 * side, (c,))
+            halo_copy(sweep, *routes[5], c).start()
+        add_near(sweep, 2 * side)
+        coef_wait(coef_recv, sweep, 1)
         partial = jnp.dot(
             masked[...],
             coefs[sweep].reshape(groups * rank, -1),
@@ -217,19 +237,21 @@
         for i in range(1, n_col):
             part_copy(sweep, i).start()
 
-        halo_wait(sweep, n_col * side)
-        halo[4].start()
-
-        @pl.when(parity == -side)
-        def _():
-            halo[6].start()
+        for c in range(CHUNKS):
+            halo_wait(sweep, n_col * side, (c,))
+            halo_copy(sweep, *routes[4], c).start()
+
+            @pl.when(parity == -side)
+            def _():
+                halo_copy(sweep, *routes[6], c).start()
 
         add_near(sweep, n_col * side)
-        halo_wait(sweep, -n_col * side)
-
-        @pl.when(parity == side)
-        def _():
-            halo[6].start()
+        for c in range(CHUNKS):
+            halo_wait(sweep, -n_col * side, (c,))
+
+            @pl.when(parity == side)
+            def _():
+                halo_copy(sweep, *routes[6], c).start()
 
         add_near(sweep, -n_col * side)
         halo_wait(sweep, 2 * side - parity)
@@ -246,8 +268,9 @@
             preferred_element_type=jnp.float32,
         )
 
-        halo_wait(sweep, -2 * side)
-        halo[7].start()
+        for c in range(CHUNKS):
+            halo_wait(sweep, -2 * side, (c,))
+            halo_copy(sweep, *routes[7], c).start()
         add_near(sweep, -2 * side)
         for d in (3 * parity, -2 * side - parity):
             halo_wait(sweep, d)
@@ -260,13 +283,11 @@
             iterate[...] = iterate[...] + DAMPING * (right[...] - total[...])
 
     for sweep in range(ITERS):
-        pltpu.make_async_copy(
-            coefs.at[sweep, pl.ds(0, groups - 1)],
-            coefs.at[sweep, pl.ds(0, groups - 1)],
-            coef_send.at[sweep],
-        ).wait()
-        for copy in copies(sweep):
-            copy.wait_send()
+        coef_wait(coef_send, sweep, 0)
+        coef_wait(coef_send, sweep, 1)
+        for route in routes:
+            for c in range(CHUNKS):
+                halo_copy(sweep, *route, c).wait_send()
         for i in range(1, n_col):
             part_copy(sweep, i).wait_send()
 
@@ -311,10 +332,10 @@
             pltpu.VMEM((ITERS, targets, rank, rhs), bf16),
             pltpu.VMEM((ITERS, targets, rank, rhs), bf16),
             dma((6,)),
-            dma((ITERS, 8)),
-            dma((ITERS, slots)),
-            dma((ITERS,)),
-            dma((ITERS,)),
+            dma((ITERS, 8, CHUNKS)),
+            dma((ITERS, slots, CHUNKS)),
+            dma((ITERS, 2)),
+            dma((ITERS, 2)),
             dma((ITERS, targets)),
             dma((ITERS, targets)),
         ],

time: 41.3 us -> 40.8 us (0.988)
  Pallas kernels: 38.6 us -> 38.1 us
    pallas_call x1, Pallas kernels: 38.6 us -> 38.1 us  [shards(): pl.pallas_call(functools.partial(kernel, sizes), out_shape=[jax.ShapeDtyp...]
where the time goes in v3:
time: 40.8 us; the launch traced here: 40.7 us
  Pallas kernels  38.1 us (93%)
  other arithmetic  1.86 us (5%)
  between operations  0.66 us (2%)
    pallas_call x1, Pallas kernels, shards(): pl.pallas_call(functools.partial(kernel, sizes), out_shape=[jax.ShapeDtyp...  38.1 us
    add x1, other arithmetic, shards(): return (last + DAMPING * residual, residual)  1.86 us

profile of v3, /device:TPU:0, one launch (start us, length us, event | category | flops | bytes accessed | tf_op | source)
XLA Modules:
  0.0 40.7 jit_solution(4811147552795521323)
XLA Ops:
  0.6 0.0 copy-start
  0.6 38.1 %shard_map.95 = (f32[1,512,128]{2,1,0:T(8,128)}, f32[1,512,128]{2,1,0:T(8,128)}) custom-call(s32[1,7]{1,0:T(1,128)} %neighbours.1, f32[1,7]{1,0:T(1,128)} %scales.1, f32[1,512,128]{2,1,0:T(8,128)} %right_hbm.1, f32[1,512,128]{2,1,0:T(8,128)} %guess_hbm.1, bf16[1,7,512,512]{3,2,1,0:T(8,128)(2,1)} %tiles_hbm.1, bf16[1,64,512]{2,1,0:T(8,128)(2,1)} %bitcast.2, ...), custom_call_target="tpu_custom_call" | custom-call | tf_op jit(solution)/shard_map/pallas_call | solution.py:316
  38.8 0.0 copy-done
  38.8 1.9 %multiply_add_fusion = (f32[1,512,128]{2,1,0:T(8,128)}, f32[1,512,128]{2,1,0:T(8,128)}) fusion(f32[1,512,128]{2,1,0:T(8,128)} %get-tuple-element.4, f32[1,512,128]{2,1,0:T(8,128)S(1)} %copy-done, f32[1,512,128]{2,1,0:T(8,128)} %get-tuple-element.5), kind=kLoop, calls=%fused_computation | loop fusion | flops 196608 | bytes 1310720 | tf_op jit(solution)/shard_map/add | solution.py:354
Async XLA Ops:
  0.6 38.2 %copy-start = (f32[1,512,128]{2,1,0:T(8,128)S(1)}, f32[1,512,128]{2,1,0:T(8,128)}, u32[]{:S(2)}) copy-start(f32[1,512,128]{2,1,0:T(8,128)} %right_hbm.1) | copy-start | bytes 786436
